TPU v7x, 32 devices: a whole 2x2x4 slice. The times are simulated.
32 devices in a mesh: inputs: 8 (over z, y), tm: 4 (over x, core).
Axes of the slice: x: 2, y: 2, z: 4, core: 2. Of those that a mesh axis runs over, the one named last changes fastest.
Arguments:
- voltages: bfloat16 [128, 131072], P('inputs', 'tm'), may hold values from -8 to 8
- pfb_taps: float32 [8, 512], replicated, may hold values from -2 to 2
Outputs:
- visibilities: float32 [256, 1, 2, 128, 128], P(('inputs', 'tm'))
All inputs are finite; a program needn't handle non-finite values.
Results may differ from a plain program's by a relative error of at most 0.002.
Values may be sent and summed in bfloat16 or wider, within the bound.
No kernel may reach another device: no remote copies, remote signals or barrier semaphores. Data moves between devices by JAX's collectives and lax.ppermute only.
A program may use at most 128 MiB of HBM per device.

v0:
```python
import jax
import jax.numpy as jnp
from jax import lax
from jax.sharding import PartitionSpec as P

F = 256
TAPS = 8
TILE = 128
FRAME = 512


def from_behind(value, axis, steps):
    count = lax.axis_size(axis)
    initial, last = (max(0, -steps), min(count, count - steps))
    return lax.ppermute(value, axis, [(source, source + steps) for source in range(initial, last)])


def dft_table(chans, length):
    rows = jnp.arange(2 * chans, dtype=jnp.int32)
    freq = rows // 2
    part = rows % 2
    samp = jnp.arange(length, dtype=jnp.int32)
    phase = freq[:, None] * samp[None, :] % length
    angle = 2.0 * jnp.pi / length * phase.astype(jnp.float32)
    vals = jnp.where(part[:, None] == 0, jnp.cos(angle), -jnp.sin(angle))
    return (vals * (1.0 / length**0.5)).astype(jnp.bfloat16)


def tile_sums(spec, scale):
    left = jnp.concatenate([spec[:, 0], spec[:, 1]], axis=-1)
    twisted = jnp.concatenate([spec[:, 1], -spec[:, 0]], axis=-1)
    count_in = left.shape[1]
    blocks = count_in // TILE
    chans = left.shape[0]
    real_rows = []
    imag_rows = []
    for first in range(blocks):
        lower = first * TILE
        cols = left[:, lower:]
        real_part = jnp.einsum(
            "cik,cjk->cij", left[:, lower : lower + TILE], cols, preferred_element_type=jnp.float32
        )
        imag_part = jnp.einsum(
            "cik,cjk->cij",
            twisted[:, lower : lower + TILE],
            cols,
            preferred_element_type=jnp.float32,
        )
        count = blocks - first
        real_rows.append(real_part.reshape(chans, TILE, count, TILE).transpose(0, 2, 1, 3))
        imag_rows.append(imag_part.reshape(chans, TILE, count, TILE).transpose(0, 2, 1, 3))
    real_all = jnp.concatenate(real_rows, axis=1)
    imag_all = jnp.concatenate(imag_rows, axis=1)
    return jnp.stack([real_all, imag_all], axis=2) * scale


def on_device(voltages, pfb_taps):
    inp_local = voltages.shape[0]
    frames_local = voltages.shape[1] // FRAME
    previous = from_behind(voltages[:, voltages.shape[1] - (TAPS - 1) * FRAME :], "tm", 1)
    extended = jnp.concatenate([previous, voltages], axis=1).reshape(
        inp_local, frames_local + TAPS - 1, FRAME
    )
    filtered = jnp.zeros((inp_local, frames_local, FRAME), jnp.float32)
    for tap in range(TAPS):
        filtered = filtered + pfb_taps[tap][None, None, :] * extended[
            :, tap : tap + frames_local, :
        ].astype(jnp.float32)
    filtered = filtered.astype(jnp.bfloat16)
    table = dft_table(F, FRAME)
    spectra = jnp.einsum("kn,itn->kit", table, filtered, preferred_element_type=jnp.float32)
    spectra = spectra.astype(jnp.bfloat16).reshape(F, 2, inp_local, frames_local)
    blocks_time = lax.axis_size("tm")
    scale = 1.0 / (frames_local * blocks_time)
    turned = lax.all_to_all(
        lax.all_to_all(spectra, "inputs", split_axis=0, concat_axis=2, tiled=True),
        "tm",
        split_axis=0,
        concat_axis=3,
        tiled=True,
    )
    return tile_sums(turned, scale)


def solution(mesh):
    in_specs = (P("inputs", "tm"), P())
    out_specs = P(("inputs", "tm"), None, None, None, None)
    return jax.shard_map(
        on_device, mesh=mesh, in_specs=in_specs, out_specs=out_specs, check_vma=False
    )
```

profile of v0, /device:TPU:0, one launch (start us, length us, event | category | flops | bytes accessed | tf_op | source)
XLA Modules:
  0.0 76.3 jit_solution(17021184768935166234)
XLA Ops:
  0.0 0.9 %slice.60 = bf16[16,3584]{1,0:T(8,128)(2,1)S(1)} slice(bf16[16,32768]{1,0:T(8,128)(2,1)} %param.2), slice={[0:16], [29184:32768]} | slice | bytes 229376 | tf_op jit(solution)/shard_map/slice | solution.py:60
  0.9 2.4 %collective-permute-start = (bf16[16,3584]{1,0:T(8,128)(2,1)S(1)}, bf16[16,3584]{1,0:T(8,128)(2,1)S(1)}, u32[]{:S(2)}, u32[]{:S(2)}) collective-permute-start(bf16[16,3584]{1,0:T(8,128)(2,1)S(1)} %slice.60), channel_id=1, source_target_pairs={{0,1},{1,2},{2,3},{4,5},{5,6},{6,7},{8,9},{9,10},{10,11},{12,13},{... | collective-permute-start | bytes 344072 | tf_op jit(solution)/shard_map/ppermute | solution.py:15
  3.3 1.0 %fusion.32 = (f32[1,512]{1,0:T(1,128)S(1)}, f32[1,512]{1,0:T(1,128)S(1)}, f32[1,512]{1,0:T(1,128)S(1)}, f32[1,512]{1,0:T(1,128)S(1)}, f32[1,512]{1,0:T(1,128)S(1...) fusion(f32[8,512]{1,0:T(8,128)} %param.3), kind=kLoop, calls=%fused_computation.48 | loop fusion | bytes 32768 | tf_op jit(solution)/shard_map/slice | solution.py:66
  4.4 0.0 collective-permute-done
  4.4 1.3 %pad_maximum_fusion = bf16[16,36352]{1,0:T(8,128)(2,1)S(1)} fusion(bf16[16,32768]{1,0:T(8,128)(2,1)} %param.2, bf16[16,3584]{1,0:T(8,128)(2,1)S(1)} %collective-permute-done), kind=kLoop, calls=%fused_computation.7 | loop fusion | flops 2326528 | bytes 2326528 | tf_op jit(solution)/shard_map/concatenate | solution.py:61
  5.7 0.7 reshape.74
  6.4 6.5 %convolution_convert_fusion = bf16[512,16,64]{0,2,1:T(8,128)(2,1)S(1)} fusion(bf16[16,71,512]{2,1,0:T(8,128)(2,1)S(1)} %reshape.74, f32[512]{0:T(512)S(1)} %bitcast.42, f32[512]{0:T(512)S(1)} %bitcast.43, f32[512]{0:T(512)S(1)} %bitcast.37, f32[512]{0:T(512)S(1)} %bitcast.38, f32[512]{0:T(512)S(1)} %bitcast.39, f32[512]{0:T(512)S(1)} %bitcast.40, ...), kind=kOutput, calls=%fused_computation.4 | convolution fusion | flops 554696704 | bytes 9456128 | tf_op jit(solution)/shard_map/kn,itn->kit/dot_general | solution.py:71
  12.9 2.0 %copy.11 = bf16[512,16,64]{2,1,0:T(8,128)(2,1)S(1)} copy(bf16[512,16,64]{0,2,1:T(8,128)(2,1)S(1)} %convolution_convert_fusion) | data formatting | bytes 2097152 | tf_op jit(solution)/shard_map/convert_element_type | solution.py:72
  15.0 1.7 %reshape.77 = bf16[8,2,32768]{2,1,0:T(2,128)(2,1)S(1)} reshape(bf16[256,2,16,64]{3,2,1,0:T(8,128)(2,1)S(1)} %bitcast.27) | data formatting | bytes 2097152
  16.7 32.5 %all_to_all.36 = bf16[8,2,32768]{2,1,0:T(2,128)(2,1)} all-to-all(bf16[8,2,32768]{2,1,0:T(2,128)(2,1)S(1)} %reshape.77), channel_id=1, replica_groups=mesh['inputs'=8,'tm'=4] {'inputs'}, dimensions={0} | all-to-all | bytes 2097152 | tf_op jit(solution)/shard_map/all_to_all | solution.py:76
  49.1 3.1 %reshape.78 = bf16[256,2,16,64]{3,2,1,0:T(8,128)(2,1)S(1)} reshape(bf16[8,2,32768]{2,1,0:T(2,128)(2,1)} %all_to_all.36) | data formatting | bytes 2097152
  52.2 2.0 %copy.12 = bf16[8,32,2,16,64]{4,3,0,2,1:T(8,128)(2,1)} copy(bf16[8,32,2,16,64]{4,3,2,1,0:T(8,128)(2,1)S(1)} %bitcast.28) | data formatting | bytes 2097152 | tf_op jit(solution)/shard_map/all_to_all | solution.py:76
  54.2 2.0 %copy.13 = bf16[32,2,128,64]{2,3,1,0:T(8,128)(2,1)S(1)} copy(bf16[32,2,128,64]{3,2,1,0:T(8,128)(2,1)} %bitcast.29) | data formatting | bytes 2097152 | tf_op jit(solution)/shard_map/all_to_all | solution.py:76
  56.2 17.4 %all_to_all.37 = bf16[32,2,128,64]{2,3,1,0:T(8,128)(2,1)S(1)} all-to-all(bf16[32,2,128,64]{2,3,1,0:T(8,128)(2,1)S(1)} %copy.13), channel_id=1, replica_groups=mesh['inputs'=8,'tm'=4] {'tm'}, dimensions={0} | all-to-all | bytes 2097152 | tf_op jit(solution)/shard_map/all_to_all | solution.py:75
  73.6 0.1 copy.14
  73.7 0.1 fusion.31
  73.8 0.2 copy.19
  74.0 0.2 copy.18
  74.3 0.4 convolution_bitcast_fusion.1
  74.7 0.4 convolution_bitcast_fusion
  75.2 0.1 maximum_multiply_fusion
  75.3 1.1 %copy.17 = f32[8,1,2,128,128]{4,3,2,1,0:T(8,128)} copy(f32[8,1,2,128,128]{4,3,0,2,1:T(8,128)S(1)} %maximum_multiply_fusion) | data formatting | bytes 2097152 | tf_op jit(solution)/shard_map/mul | solution.py:54
  (3 shorter events, 0.0 us)
Async XLA Ops:
  0.9 3.5 %collective-permute-start = (bf16[16,3584]{1,0:T(8,128)(2,1)S(1)}, bf16[16,3584]{1,0:T(8,128)(2,1)S(1)}, u32[]{:S(2)}, u32[]{:S(2)}) collective-permute-start(bf16[16,3584]{1,0:T(8,128)(2,1)S(1)} %slice.60), channel_id=1, source_target_pairs={{0,1},{1,2},{2,3},{4,5},{5,6},{6,7},{8,9},{9,10},{10,11},{12,13},{... | collective-permute-start | bytes 344072 | tf_op jit(solution)/shard_map/ppermute | solution.py:15
where the time goes:
time: 76.7 us; the launch traced here: 76.3 us
  blocking collectives  49.9 us (65%)
  local copies, waits for them, and re-layouts  15.1 us (20%)
  matrix products  7.4 us (10%)
  starting transfers between devices  2.39 us (3%)
  other arithmetic  1.43 us (2%)
    all_to_all x1, blocking collectives, on_device(): lax.all_to_all(spectra, 'inputs', split_axis=0, concat_axis=2, tiled=True)  32.5 us
    all_to_all x1, blocking collectives, on_device(): lax.all_to_all(lax.all_to_all(spectra, 'inputs', split_axis=0, concat_axi...  17.4 us
    dot_general x1, matrix products, on_device(): jnp.einsum('kn,itn->kit', table, filtered, preferred_element_type=jnp.flo...  6.55 us
    unnamed x4, local copies, waits for them, and re-layouts  5.2 us
    all_to_all x2, local copies, waits for them, and re-layouts, on_device(): lax.all_to_all(spectra, 'inputs', split_axis=0, concat_axis=2, tiled=True)  3.96 us
    ppermute x1, starting transfers between devices, from_behind(): lax.ppermute(value, axis, [(source, source + steps) for source in range(i...  2.39 us
    convert_element_type x1, local copies, waits for them, and re-layouts, on_device(): spectra.astype(jnp.bfloat16).reshape(F, 2, inp_local, frames_local)  2.03 us
  transfers between devices with their start and end apart: 1, of which 0 were waited for; matrix products, arithmetic and copies ran while one was open for 1% of the time, Pallas kernels for 0%

commit v1 on v0

--- a/solution.py
+++ b/solution.py
@@ -1,3 +1,4 @@
+import functools
 import jax
 import jax.numpy as jnp
 from jax import lax
@@ -7,6 +8,37 @@
 TAPS = 8
 TILE = 128
 FRAME = 512
+
+
+def return_all_the_shapes(field, at_axis, z):
+    newest, near = (field.shape[:at_axis], field.shape[at_axis + 1 :])
+    return jnp.moveaxis(field.reshape(*newest, z, -1, *near), at_axis, 0)
+
+
+def detail_the_unit(mat, d_out):
+    f_next = list(mat.shape[1:])
+    f_next[d_out] *= mat.shape[0]
+    return jnp.moveaxis(mat, 0, d_out).reshape(f_next)
+
+
+def prepare_pools(block_here, lane_axis, t0, w_in):
+    now = lax.axis_size(lane_axis)
+    front = lax.axis_index(lane_axis)
+    row_out, main = (now, front)
+    a_now = return_all_the_shapes(block_here, t0, row_out)
+    crops = [a_now[main]]
+    for c in range(1, row_out):
+        taken_in = a_now[main ^ c]
+        crops.append(
+            lax.ppermute(
+                taken_in, axis_name=lane_axis, perm=[(to_i, to_i ^ c) for to_i in range(row_out)]
+            )
+        )
+    a_now = jnp.stack(crops)[main ^ jnp.arange(row_out)]
+    return detail_the_unit(a_now, w_in)
+
+
+use_the_series_all = functools.partial(prepare_pools, lane_axis="tm", t0=0, w_in=3)
 
 
 def from_behind(value, axis, steps):
@@ -72,12 +104,8 @@
     spectra = spectra.astype(jnp.bfloat16).reshape(F, 2, inp_local, frames_local)
     blocks_time = lax.axis_size("tm")
     scale = 1.0 / (frames_local * blocks_time)
-    turned = lax.all_to_all(
-        lax.all_to_all(spectra, "inputs", split_axis=0, concat_axis=2, tiled=True),
-        "tm",
-        split_axis=0,
-        concat_axis=3,
-        tiled=True,
+    turned = use_the_series_all(
+        lax.all_to_all(spectra, "inputs", split_axis=0, concat_axis=2, tiled=True)
     )
     return tile_sums(turned, scale)
 

time: 76.7 us -> 71.6 us (0.934)
  blocking collectives: 49.9 us -> 0 us
  waiting for transfers between devices: 0.01 us -> 37.5 us
  starting transfers between devices: 2.39 us -> 11.5 us
  local copies, waits for them, and re-layouts: 15.1 us -> 12.8 us
    all_to_all x2 -> x0, blocking collectives: 49.9 us -> none  [the longest x1 32.5 us: on_device(): lax.all_to_all(spectra, 'inputs', split_axis=0, concat_axis=2, tiled=True)]
    all_to_all x0 -> x1, waiting for transfers between devices: none -> 26.5 us  [on_device(): lax.all_to_all(spectra, 'inputs', split_axis=0, concat_axis=2, tiled=True)]
    ppermute x0 -> x3, waiting for transfers between devices: none -> 11 us  [prepare_pools(): lax.ppermute(taken_in, axis_name=lane_axis, perm=[(to_i, to_i ^ c) for to...]
    all_to_all x0 -> x1, starting transfers between devices: none -> 6.65 us  [on_device(): lax.all_to_all(spectra, 'inputs', split_axis=0, concat_axis=2, tiled=True)]
    all_to_all x2 -> x1, local copies, waits for them, and re-layouts: 3.96 us -> 0.61 us  [on_device(): lax.all_to_all(spectra, 'inputs', split_axis=0, concat_axis=2, tiled=True)]
    ppermute x0 -> x3, starting transfers between devices: none -> 2.47 us  [prepare_pools(): lax.ppermute(taken_in, axis_name=lane_axis, perm=[(to_i, to_i ^ c) for to...]
    dynamic_slice x0 -> x4, local copies, waits for them, and re-layouts: none -> 0.8 us  [the longest x3 0.66 us: prepare_pools(): taken_in = a_now[main ^ c]]
    unnamed x4 -> x5, local copies, waits for them, and re-layouts: 5.2 us -> 4.73 us
  transfers between devices with their start and end apart: 1 -> 5, of which waited for: 0 -> 3; matrix products, arithmetic and copies ran while one was open for 1% -> 2% of each run, Pallas kernels for 0% -> 0%
where the time goes in v1:
time: 71.6 us; the launch traced here: 71 us
  waiting for transfers between devices  37.5 us (52%)
  local copies, waits for them, and re-layouts  12.8 us (18%)
  starting transfers between devices  11.5 us (16%)
  matrix products  7.41 us (10%)
  other arithmetic  1.58 us (2%)
    all_to_all x1, waiting for transfers between devices, on_device(): lax.all_to_all(spectra, 'inputs', split_axis=0, concat_axis=2, tiled=True)  26.5 us
    ppermute x3, waiting for transfers between devices, prepare_pools(): lax.ppermute(taken_in, axis_name=lane_axis, perm=[(to_i, to_i ^ c) for to...  11 us
    all_to_all x1, starting transfers between devices, on_device(): lax.all_to_all(spectra, 'inputs', split_axis=0, concat_axis=2, tiled=True)  6.65 us
    dot_general x1, matrix products, on_device(): jnp.einsum('kn,itn->kit', table, filtered, preferred_element_type=jnp.flo...  6.55 us
    unnamed x5, local copies, waits for them, and re-layouts  4.73 us
    ppermute x3, starting transfers between devices, prepare_pools(): lax.ppermute(taken_in, axis_name=lane_axis, perm=[(to_i, to_i ^ c) for to...  2.47 us
    ppermute x1, starting transfers between devices, from_behind(): lax.ppermute(value, axis, [(source, source + steps) for source in range(i...  2.39 us
    convert_element_type x1, local copies, waits for them, and re-layouts, on_device(): spectra.astype(jnp.bfloat16).reshape(F, 2, inp_local, frames_local)  2.03 us
  transfers between devices with their start and end apart: 5, of which 3 were waited for; matrix products, arithmetic and copies ran while one was open for 2% of the time, Pallas kernels for 0%

profile of v1, /device:TPU:0, one launch (start us, length us, event | category | flops | bytes accessed | tf_op | source)
XLA Modules:
  0.0 71.0 jit_solution(3748333076297289736)
XLA Ops:
  0.0 0.9 %slice.60 = bf16[16,3584]{1,0:T(8,128)(2,1)S(1)} slice(bf16[16,32768]{1,0:T(8,128)(2,1)} %param.2), slice={[0:16], [29184:32768]} | slice | bytes 229376 | tf_op jit(solution)/shard_map/slice | solution.py:92
  0.9 2.4 %collective-permute-start = (bf16[16,3584]{1,0:T(8,128)(2,1)S(1)}, bf16[16,3584]{1,0:T(8,128)(2,1)S(1)}, u32[]{:S(2)}, u32[]{:S(2)}) collective-permute-start(bf16[16,3584]{1,0:T(8,128)(2,1)S(1)} %slice.60), channel_id=1, source_target_pairs={{0,1},{1,2},{2,3},{4,5},{5,6},{6,7},{8,9},{9,10},{10,11},{12,13},{... | collective-permute-start | bytes 344072 | tf_op jit(solution)/shard_map/ppermute | solution.py:47
  3.3 1.0 %fusion.33 = (f32[1,512]{1,0:T(1,128)S(1)}, f32[1,512]{1,0:T(1,128)S(1)}, f32[1,512]{1,0:T(1,128)S(1)}, f32[1,512]{1,0:T(1,128)S(1)}, f32[1,512]{1,0:T(1,128)S(1...) fusion(f32[8,512]{1,0:T(8,128)} %param.3), kind=kLoop, calls=%fused_computation.57 | loop fusion | bytes 32768 | tf_op jit(solution)/shard_map/slice | solution.py:98
  4.4 1.3 %pad_maximum_fusion = bf16[16,36352]{1,0:T(8,128)(2,1)S(1)} fusion(bf16[16,32768]{1,0:T(8,128)(2,1)} %param.2, bf16[16,3584]{1,0:T(8,128)(2,1)S(1)} %collective-permute-done), kind=kLoop, calls=%fused_computation.8 | loop fusion | flops 2326528 | bytes 2326528 | tf_op jit(solution)/shard_map/concatenate | solution.py:93
  5.7 0.7 reshape.97
  6.4 6.5 %convolution_convert_fusion = bf16[512,16,64]{0,2,1:T(8,128)(2,1)S(1)} fusion(bf16[16,71,512]{2,1,0:T(8,128)(2,1)S(1)} %reshape.97, f32[512]{0:T(512)S(1)} %bitcast.54, f32[512]{0:T(512)S(1)} %bitcast.55, f32[512]{0:T(512)S(1)} %bitcast.49, f32[512]{0:T(512)S(1)} %bitcast.50, f32[512]{0:T(512)S(1)} %bitcast.51, f32[512]{0:T(512)S(1)} %bitcast.52, ...), kind=kOutput, calls=%fused_computation.5 | convolution fusion | flops 554696704 | bytes 9456128 | tf_op jit(solution)/shard_map/kn,itn->kit/dot_general | solution.py:103
  12.9 2.0 %copy.4 = bf16[512,16,64]{2,1,0:T(8,128)(2,1)S(1)} copy(bf16[512,16,64]{0,2,1:T(8,128)(2,1)S(1)} %convolution_convert_fusion) | data formatting | bytes 2097152 | tf_op jit(solution)/shard_map/convert_element_type | solution.py:104
  15.0 2.7 %reshape.110 = bf16[8,2,32768]{2,1,0:T(2,128)(2,1)} reshape(bf16[256,2,16,64]{3,2,1,0:T(8,128)(2,1)S(1)} %bitcast.34) | data formatting | bytes 2097152
  17.6 6.7 %all-to-all-start = ((bf16[8,2,32768]{2,1,0:T(2,128)(2,1)}), bf16[8,2,32768]{2,1,0:T(2,128)(2,1)S(1)}, u32[]{:S(2)}, u32[]{:S(2)}) async-start(bf16[8,2,32768]{2,1,0:T(2,128)(2,1)} %reshape.110), calls=%async_computation | async-start | bytes 2097152 | tf_op jit(solution)/shard_map/all_to_all | solution.py:108
  24.3 26.5 %all-to-all-done = bf16[8,2,32768]{2,1,0:T(2,128)(2,1)S(1)} async-done(((bf16[8,2,32768]{2,1,0:T(2,128)(2,1)}), bf16[8,2,32768]{2,1,0:T(2,128)(2,1)S(1)}, u32[]{:S(2)}, u32[]{:S(2)}) %all-to-all-start) | async-done | bytes 1048608 | tf_op jit(solution)/shard_map/all_to_all | solution.py:108
  50.8 1.4 %reshape.111 = bf16[256,2,16,64]{3,2,1,0:T(8,128)(2,1)S(1)} reshape(bf16[8,2,32768]{2,1,0:T(2,128)(2,1)S(1)} %all-to-all-done) | data formatting | bytes 2097152
  52.2 0.6 copy.5
  52.8 0.1 constant_dynamic-slice_fusion.3
  53.0 0.2 copy.7
  53.2 1.0 %collective-permute-start.1 = (bf16[8,2,128,64]{2,3,1,0:T(8,128)(2,1)S(1)}, bf16[8,2,128,64]{2,3,1,0:T(8,128)(2,1)S(1)}, u32[]{:S(2)}, u32[]{:S(2)}) collective-permute-start(bf16[8,2,128,64]{2,3,1,0:T(8,128)(2,1)S(1)} %bitcast.42), channel_id=1, source_target_pairs={{0,1},{1,0},{2,3},{3,2},{4,5},{5,4},{6,7},{7,6},{8,9},{9,8},{10,11... | collective-permute-start | bytes 786440 | tf_op jit(solution)/shard_map/ppermute | solution.py:33
  54.2 0.2 copy.8
  54.4 0.7 %collective-permute-start.2 = (bf16[8,2,128,64]{2,3,1,0:T(8,128)(2,1)S(1)}, bf16[8,2,128,64]{2,3,1,0:T(8,128)(2,1)S(1)}, u32[]{:S(2)}, u32[]{:S(2)}) collective-permute-start(bf16[8,2,128,64]{2,3,1,0:T(8,128)(2,1)S(1)} %bitcast.43), channel_id=1, source_target_pairs={{0,2},{1,3},{2,0},{3,1},{4,6},{5,7},{6,4},{7,5},{8,10},{9,11},{10,... | collective-permute-start | bytes 786440 | tf_op jit(solution)/shard_map/ppermute | solution.py:33
  55.1 0.2 copy.9
  55.4 0.8 %collective-permute-start.3 = (bf16[8,2,128,64]{2,3,1,0:T(8,128)(2,1)S(1)}, bf16[8,2,128,64]{2,3,1,0:T(8,128)(2,1)S(1)}, u32[]{:S(2)}, u32[]{:S(2)}) collective-permute-start(bf16[8,2,128,64]{2,3,1,0:T(8,128)(2,1)S(1)} %bitcast.44), channel_id=1, source_target_pairs={{0,3},{1,2},{2,1},{3,0},{4,7},{5,6},{6,5},{7,4},{8,11},{9,10},{10,... | collective-permute-start | bytes 786440 | tf_op jit(solution)/shard_map/ppermute | solution.py:33
  56.1 0.2 copy.14
  56.4 7.3 %collective-permute-done.2 = bf16[8,2,128,64]{2,3,1,0:T(8,128)(2,1)S(1)} collective-permute-done((bf16[8,2,128,64]{2,3,1,0:T(8,128)(2,1)S(1)}, bf16[8,2,128,64]{2,3,1,0:T(8,128)(2,1)S(1)}, u32[]{:S(2)}, u32[]{:S(2)}) %collective-permute-start.2) | collective-permute-done | bytes 262176 | tf_op jit(solution)/shard_map/ppermute | solution.py:33
  63.7 3.7 %collective-permute-done.3 = bf16[8,2,128,64]{2,3,1,0:T(8,128)(2,1)S(1)} collective-permute-done((bf16[8,2,128,64]{2,3,1,0:T(8,128)(2,1)S(1)}, bf16[8,2,128,64]{2,3,1,0:T(8,128)(2,1)S(1)}, u32[]{:S(2)}, u32[]{:S(2)}) %collective-permute-start.3) | collective-permute-done | bytes 262176 | tf_op jit(solution)/shard_map/ppermute | solution.py:33
  67.4 0.1 pad_maximum_fusion.1
  67.5 0.7 %gather_fusion = bf16[4,8,2,128,64]{3,4,2,1,0:T(8,128)(2,1)S(1)} fusion(bf16[4,8,2,128,64]{3,4,2,1,0:T(8,128)(2,1)S(1)} %pad_maximum_fusion.1, s32[1024]{0:T(1024)S(1)} %pad_clamp_fusion), kind=kCustom, calls=%fused_computation | custom fusion | bytes 2097168 | tf_op jit(solution)/shard_map/gather | solution.py:37
  68.2 0.1 copy.10
  68.3 0.1 fusion.32
  68.4 0.2 copy.15
  68.7 0.2 copy.16
  68.9 0.4 convolution_bitcast_fusion.1
  69.4 0.4 convolution_bitcast_fusion
  69.8 0.1 maximum_multiply_fusion
  69.9 1.1 %copy.13 = f32[8,1,2,128,128]{4,3,2,1,0:T(8,128)} copy(f32[8,1,2,128,128]{4,3,0,2,1:T(8,128)S(1)} %maximum_multiply_fusion) | data formatting | bytes 2097152 | tf_op jit(solution)/shard_map/mul | solution.py:86
  (7 shorter events, 0.1 us)
Async XLA Ops:
  0.9 3.5 %collective-permute-start = (bf16[16,3584]{1,0:T(8,128)(2,1)S(1)}, bf16[16,3584]{1,0:T(8,128)(2,1)S(1)}, u32[]{:S(2)}, u32[]{:S(2)}) collective-permute-start(bf16[16,3584]{1,0:T(8,128)(2,1)S(1)} %slice.60), channel_id=1, source_target_pairs={{0,1},{1,2},{2,3},{4,5},{5,6},{6,7},{8,9},{9,10},{10,11},{12,13},{... | collective-permute-start | bytes 344072 | tf_op jit(solution)/shard_map/ppermute | solution.py:47
  17.6 33.1 %all-to-all-start = ((bf16[8,2,32768]{2,1,0:T(2,128)(2,1)}), bf16[8,2,32768]{2,1,0:T(2,128)(2,1)S(1)}, u32[]{:S(2)}, u32[]{:S(2)}) async-start(bf16[8,2,32768]{2,1,0:T(2,128)(2,1)} %reshape.110), calls=%async_computation | async-start | bytes 2097152 | tf_op jit(solution)/shard_map/all_to_all | solution.py:108
  53.2 3.2 %collective-permute-start.1 = (bf16[8,2,128,64]{2,3,1,0:T(8,128)(2,1)S(1)}, bf16[8,2,128,64]{2,3,1,0:T(8,128)(2,1)S(1)}, u32[]{:S(2)}, u32[]{:S(2)}) collective-permute-start(bf16[8,2,128,64]{2,3,1,0:T(8,128)(2,1)S(1)} %bitcast.42), channel_id=1, source_target_pairs={{0,1},{1,0},{2,3},{3,2},{4,5},{5,4},{6,7},{7,6},{8,9},{9,8},{10,11... | collective-permute-start | bytes 786440 | tf_op jit(solution)/shard_map/ppermute | solution.py:33
  54.4 9.2 %collective-permute-start.2 = (bf16[8,2,128,64]{2,3,1,0:T(8,128)(2,1)S(1)}, bf16[8,2,128,64]{2,3,1,0:T(8,128)(2,1)S(1)}, u32[]{:S(2)}, u32[]{:S(2)}) collective-permute-start(bf16[8,2,128,64]{2,3,1,0:T(8,128)(2,1)S(1)} %bitcast.43), channel_id=1, source_target_pairs={{0,2},{1,3},{2,0},{3,1},{4,6},{5,7},{6,4},{7,5},{8,10},{9,11},{10,... | collective-permute-start | bytes 786440 | tf_op jit(solution)/shard_map/ppermute | solution.py:33
  55.4 12.0 %collective-permute-start.3 = (bf16[8,2,128,64]{2,3,1,0:T(8,128)(2,1)S(1)}, bf16[8,2,128,64]{2,3,1,0:T(8,128)(2,1)S(1)}, u32[]{:S(2)}, u32[]{:S(2)}) collective-permute-start(bf16[8,2,128,64]{2,3,1,0:T(8,128)(2,1)S(1)} %bitcast.44), channel_id=1, source_target_pairs={{0,3},{1,2},{2,1},{3,0},{4,7},{5,6},{6,5},{7,4},{8,11},{9,10},{10,... | collective-permute-start | bytes 786440 | tf_op jit(solution)/shard_map/ppermute | solution.py:33
